TPU v7x, 256 devices: a whole 4x4x8 slice. The times are simulated.
256 devices in a mesh: energy: 128 (over y_lo, x, z, core), mode: 2 (over y_hi).
Axes of the slice: x: 4, y: 4 (y_hi: 2, y_lo: 2; y = y_hi * 2 + y_lo), z: 8, core: 2. Of those that a mesh axis runs over, the one named last changes fastest.
Arguments:
- spectral: float32 [128, 896, 896], P('energy', 'mode'), may hold values from -6 to 6
- coupling: bfloat16 [2, 896, 896], P('mode'), may hold values from -0.1875 to 0.1875
- offsets: int32 [2], P('mode'), may hold values from 1 to 2, as said below
- occupation: int32 [2, 128], P('mode', 'energy'), may hold values from 0 to 3
Outputs:
- self_energy: float32 [128, 896, 896], P('energy', 'mode')
Inputs may be any that keep to these rules, and one draw needn't show every extreme that they name: `offsets`: each offset from 1 to 2 belongs to exactly 1 modes.
All inputs are finite; a program needn't handle non-finite values.
Results may differ from a plain program's by a relative error of at most 0.0041.
Values sent between devices are 32-bit elements; how exact they have to be, the bound alone decides.
A program may use at most 64 MiB of HBM per device.

v0:
```python
import jax
import jax.numpy as jnp
from jax import lax
from jax.sharding import PartitionSpec as P

KMAX = 2


def passed_along(value, axis, steps):
    count = lax.axis_size(axis)
    first, last = (max(0, -steps), min(count, count - steps))
    return lax.ppermute(value, axis, [(source, source + steps) for source in range(first, last)])


def split_up(value, dim, devices):
    shape = value.shape
    parts = value.reshape(*shape[:dim], devices, shape[dim] // devices, *shape[dim + 1 :])
    return jnp.moveaxis(parts, dim, 0)


def summed_on_arrival(value, axis, dim):
    parts = split_up(value, dim, lax.axis_size(axis))
    arrived = lax.all_to_all(parts, axis, split_axis=0, concat_axis=0, tiled=True)
    return arrived.sum(axis=0)


def collect_rim(own_block, max_offset):
    per_device = own_block.shape[0]
    farthest = -(-max_offset // per_device)
    requests = []
    for distance in range(farthest, 0, -1):
        requests.append((distance, max(0, distance * per_device - max_offset), per_device))
    for distance in range(1, farthest + 1):
        requests.append((-distance, 0, min(per_device, max_offset - (distance - 1) * per_device)))
    lower_parts = []
    upper_parts = []
    for shift_by, first_row, last_row in requests:
        arrived = passed_along(own_block, "energy", shift_by)
        if shift_by > 0:
            lower_parts.append(arrived)
        else:
            upper_parts.append(arrived)
    return jnp.concatenate(lower_parts + [own_block] + upper_parts, axis=0)


def shards(spectral, coupling, offsets, occupation):
    max_offset = KMAX
    full_block = lax.all_gather(spectral, "mode", axis=1, tiled=True)
    window = collect_rim(full_block, max_offset)
    per_device = spectral.shape[0]
    window_len = window.shape[0]
    position = lax.broadcasted_iota(jnp.int32, (1, per_device, window_len), 2)
    energy_pos = lax.broadcasted_iota(jnp.int32, (1, per_device, window_len), 1) + max_offset
    offset_col = offsets[:, None, None]
    emission = (occupation + 1).astype(jnp.float32)[:, :, None]
    absorption = occupation.astype(jnp.float32)[:, :, None]
    weights_table = jnp.where(position == energy_pos - offset_col, emission, 0.0)
    weights_table = weights_table + jnp.where(position == energy_pos + offset_col, absorption, 0.0)
    combined = jnp.einsum(
        "mew,wij->meij", weights_table, window, precision=lax.Precision.HIGHEST
    ).astype(jnp.bfloat16)
    coupled = jnp.einsum(
        "mij,mejk->meik", coupling, combined, preferred_element_type=jnp.float32
    ).astype(jnp.bfloat16)
    partial_sum = jnp.einsum("meik,mlk->eil", coupled, coupling, preferred_element_type=jnp.float32)
    modes_all = coupling.shape[0] * lax.axis_size("mode")
    summed = summed_on_arrival(partial_sum, "mode", 1)
    return summed / modes_all


def solution(mesh):
    return jax.shard_map(
        shards,
        mesh=mesh,
        in_specs=(P("energy", "mode", None), P("mode", None, None), P("mode"), P("mode", "energy")),
        out_specs=P("energy", "mode", None),
        check_vma=False,
    )
```

profile of v0, /device:TPU:96, one launch (start us, length us, event | category | flops | bytes accessed | tf_op | source)
XLA Modules:
  0.0 263.5 jit_solution(1662050244572922762)
XLA Ops:
  6.5 0.0 copy-start
  6.5 0.0 all-gather.2.cloned.1.call-start
  6.5 0.7 all-gather.2.cloned.1.call-update
  7.3 56.1 %all-gather.2.cloned.1.call-done = f32[1,896,896]{2,1,0:T(8,128)} async-done(((f32[1,448,896]{2,1,0:T(8,128)}), f32[1,896,896]{2,1,0:T(8,128)}) %all-gather.2.cloned.1.call-update) | async-done | bytes 3211280 | tf_op jit(solution)/shard_map/all_gather | solution.py:48
  63.4 4.7 %collective-permute-start = (f32[1,896,896]{2,1,0:T(8,128)}, f32[1,896,896]{2,1,0:T(8,128)S(1)}, u32[]{:S(2)}, u32[]{:S(2)}) collective-permute-start(f32[1,896,896]{2,1,0:T(8,128)} %all-gather.2.cloned.1.call-done), channel_id=1, source_target_pairs={{0,4},{2,6},{4,8},{6,10},{8,12},{10,14},{12,16},{14,18},{16,20},{1... | collective-permute-start | bytes 9633800 | tf_op jit(solution)/shard_map/ppermute | solution.py:12
  68.0 1.9 collective-permute-start.1
  70.0 3.6 %collective-permute-start.2 = (f32[1,896,896]{2,1,0:T(8,128)}, f32[1,896,896]{2,1,0:T(8,128)S(1)}, u32[]{:S(2)}, u32[]{:S(2)}) collective-permute-start(f32[1,896,896]{2,1,0:T(8,128)} %all-gather.2.cloned.1.call-done), channel_id=1, source_target_pairs={{2,0},{4,2},{6,4},{8,6},{10,8},{12,10},{14,12},{16,14},{18,16},{20... | collective-permute-start | bytes 9633800 | tf_op jit(solution)/shard_map/ppermute | solution.py:12
  73.6 1.9 collective-permute-start.3
  76.8 61.4 %collective-permute-done = f32[1,896,896]{2,1,0:T(8,128)S(1)} collective-permute-done((f32[1,896,896]{2,1,0:T(8,128)}, f32[1,896,896]{2,1,0:T(8,128)S(1)}, u32[]{:S(2)}, u32[]{:S(2)}) %collective-permute-start) | collective-permute-done | bytes 3211296 | tf_op jit(solution)/shard_map/ppermute | solution.py:12
  138.2 0.2 constant_dynamic-update-slice_fusion.4
  138.4 0.0 copy-start.1
  138.5 32.7 %collective-permute-done.1 = f32[1,896,896]{2,1,0:T(8,128)S(1)} collective-permute-done((f32[1,896,896]{2,1,0:T(8,128)}, f32[1,896,896]{2,1,0:T(8,128)S(1)}, u32[]{:S(2)}, u32[]{:S(2)}) %collective-permute-start.1) | collective-permute-done | bytes 3211296 | tf_op jit(solution)/shard_map/ppermute | solution.py:12
  171.1 0.2 constant_dynamic-update-slice_fusion.3
  171.3 0.0 copy-done.1
  171.3 0.2 constant_dynamic-update-slice_fusion.2
  171.5 0.0 collective-permute-done.2
  171.6 0.2 constant_dynamic-update-slice_fusion.1
  171.8 8.6 %collective-permute-done.3 = f32[1,896,896]{2,1,0:T(8,128)S(1)} collective-permute-done((f32[1,896,896]{2,1,0:T(8,128)}, f32[1,896,896]{2,1,0:T(8,128)S(1)}, u32[]{:S(2)}, u32[]{:S(2)}) %collective-permute-start.3) | collective-permute-done | bytes 3211296 | tf_op jit(solution)/shard_map/ppermute | solution.py:12
  180.4 0.2 constant_dynamic-update-slice_fusion
  180.6 34.3 %fusion = bf16[1,896,896]{2,0,1:T(2,128)(2,1)S(1)} fusion(f32[5,896,896]{2,1,0:T(8,128)S(1)} %constant_dynamic-update-slice_fusion, f32[]{:T(128)} %bitcast.3, s32[]{:T(128)} %bitcast.2, f32[]{:T(128)} %bitcast.1, s32[]{:T(128)} %bitcast), kind=kOutput, calls=%fused_computation | convolution fusion | flops 48168984 | bytes 17661968 | tf_op jit(solution)/shard_map/mew,wij->meij/dot_general | solution.py:59
  214.9 0.0 copy-done
  215.0 2.0 convolution_convert_fusion
  217.0 2.0 convolution_bitcast_fusion
  219.0 34.2 %all_to_all.5 = f32[2,1,448,896]{3,2,1,0:T(8,128)} all-to-all(f32[2,1,448,896]{3,2,1,0:T(8,128)S(1)} %convolution_bitcast_fusion), channel_id=1, replica_groups=mesh['energy'=128,'mode'=2] {'mode'}, dimensions={0} | all-to-all | bytes 6422528 | tf_op jit(solution)/shard_map/all_to_all | solution.py:23
  253.2 2.3 reduce_sum.9
  255.4 1.3 multiply_bitcast_fusion
Async XLA Ops:
  6.5 208.4 %copy-start = (bf16[1,896,896]{2,1,0:T(8,128)(2,1)S(1)}, bf16[1,896,896]{2,1,0:T(8,128)(2,1)}, u32[]{:S(2)}) copy-start(bf16[1,896,896]{2,1,0:T(8,128)(2,1)} %param.5) | copy-start | bytes 4816900
  6.5 56.8 %all-gather.2.cloned.1.call-start = ((), (), s32[]{:S(2)}) async-start(), calls=%async_computation.1 | async-start | bytes 4816896 | tf_op jit(solution)/shard_map/all_gather | solution.py:48
  63.4 74.9 %collective-permute-start = (f32[1,896,896]{2,1,0:T(8,128)}, f32[1,896,896]{2,1,0:T(8,128)S(1)}, u32[]{:S(2)}, u32[]{:S(2)}) collective-permute-start(f32[1,896,896]{2,1,0:T(8,128)} %all-gather.2.cloned.1.call-done), channel_id=1, source_target_pairs={{0,4},{2,6},{4,8},{6,10},{8,12},{10,14},{12,16},{14,18},{16,20},{1... | collective-permute-start | bytes 9633800 | tf_op jit(solution)/shard_map/ppermute | solution.py:12
  68.0 103.1 %collective-permute-start.1 = (f32[1,896,896]{2,1,0:T(8,128)}, f32[1,896,896]{2,1,0:T(8,128)S(1)}, u32[]{:S(2)}, u32[]{:S(2)}) collective-permute-start(f32[1,896,896]{2,1,0:T(8,128)} %all-gather.2.cloned.1.call-done), channel_id=1, source_target_pairs={{0,2},{2,4},{4,6},{6,8},{8,10},{10,12},{12,14},{14,16},{16,18},{18... | collective-permute-start | bytes 9633800 | tf_op jit(solution)/shard_map/ppermute | solution.py:12
  70.0 101.6 %collective-permute-start.2 = (f32[1,896,896]{2,1,0:T(8,128)}, f32[1,896,896]{2,1,0:T(8,128)S(1)}, u32[]{:S(2)}, u32[]{:S(2)}) collective-permute-start(f32[1,896,896]{2,1,0:T(8,128)} %all-gather.2.cloned.1.call-done), channel_id=1, source_target_pairs={{2,0},{4,2},{6,4},{8,6},{10,8},{12,10},{14,12},{16,14},{18,16},{20... | collective-permute-start | bytes 9633800 | tf_op jit(solution)/shard_map/ppermute | solution.py:12
  73.6 106.8 %collective-permute-start.3 = (f32[1,896,896]{2,1,0:T(8,128)}, f32[1,896,896]{2,1,0:T(8,128)S(1)}, u32[]{:S(2)}, u32[]{:S(2)}) collective-permute-start(f32[1,896,896]{2,1,0:T(8,128)} %all-gather.2.cloned.1.call-done), channel_id=1, source_target_pairs={{4,0},{6,2},{8,4},{10,6},{12,8},{14,10},{16,12},{18,14},{20,16},{2... | collective-permute-start | bytes 9633800 | tf_op jit(solution)/shard_map/ppermute | solution.py:12
  138.4 32.9 %copy-start.1 = (f32[1,896,896]{2,1,0:T(8,128)S(1)}, f32[1,896,896]{2,1,0:T(8,128)}, u32[]{:S(2)}) copy-start(f32[1,896,896]{2,1,0:T(8,128)} %all-gather.2.cloned.1.call-done) | copy-start | bytes 9633796
Sparse Core Ops, SparseCore 0:
  9.2 54.1 all-gather.1
where the time goes:
time: 264 us
  waiting for transfers between devices  160 us (61%)
  matrix products  38.3 us (15%)
  blocking collectives  34.2 us (13%)
  between operations  14.8 us (6%)
  starting transfers between devices  12.1 us (5%)
  other arithmetic  3.54 us (1%)
    ppermute x4, waiting for transfers between devices, passed_along(): lax.ppermute(value, axis, [(source, source + steps) for source in range(f...  103 us
    all_gather x1, waiting for transfers between devices, shards(): full_block = lax.all_gather(spectral, 'mode', axis=1, tiled=True)  56.1 us
    dot_general x1, matrix products, shards(): jnp.einsum('mew,wij->meij', weights_table, window, precision=lax.Precisio...  34.3 us
    all_to_all x1, blocking collectives, summed_on_arrival(): lax.all_to_all(parts, axis, split_axis=0, concat_axis=0, tiled=True)  34.2 us
    ppermute x4, starting transfers between devices, passed_along(): lax.ppermute(value, axis, [(source, source + steps) for source in range(f...  12.1 us
  transfers between devices with their start and end apart: 5, of which 4 were waited for; matrix products, arithmetic and copies ran while one was open for 0% of the time, Pallas kernels for 0%

commit v1 on v0

--- a/solution.py
+++ b/solution.py
@@ -45,7 +45,9 @@
 
 def shards(spectral, coupling, offsets, occupation):
     max_offset = KMAX
-    full_block = lax.all_gather(spectral, "mode", axis=1, tiled=True)
+    full_block = jnp.concatenate(
+        lax.all_to_all(jnp.stack([spectral] * lax.axis_size("mode")), "mode", 0, 0), axis=1
+    )
     window = collect_rim(full_block, max_offset)
     per_device = spectral.shape[0]
     window_len = window.shape[0]

time: 264 us -> 237 us (0.90)
  waiting for transfers between devices: 160 us -> 103 us
  blocking collectives: 34.2 us -> 75 us
  between operations: 14.8 us -> 1.4 us
    all_gather x1 -> x0, waiting for transfers between devices: 56.1 us -> none  [shards(): full_block = lax.all_gather(spectral, 'mode', axis=1, tiled=True)]
    all_to_all x0 -> x1, blocking collectives: none -> 42.5 us  [shards(): lax.all_to_all(jnp.stack([spectral] * lax.axis_size('mode')), 'mode', 0, 0)]
  transfers between devices with their start and end apart: 5 -> 4, of which waited for: 4 -> 3; matrix products, arithmetic and copies ran while one was open for 0% -> 0% of each run, Pallas kernels for 0% -> 0%
where the time goes in v1:
time: 237 us
  waiting for transfers between devices  103 us (43%)
  blocking collectives  75 us (32%)
  matrix products  38.3 us (16%)
  starting transfers between devices  12.5 us (5%)
  other arithmetic  5.8 us (2%)
    ppermute x4, waiting for transfers between devices, passed_along(): lax.ppermute(value, axis, [(source, source + steps) for source in range(f...  103 us
    all_to_all x1, blocking collectives, shards(): lax.all_to_all(jnp.stack([spectral] * lax.axis_size('mode')), 'mode', 0, 0)  42.5 us
    dot_general x1, matrix products, shards(): jnp.einsum('mew,wij->meij', weights_table, window, precision=lax.Precisio...  34.3 us
    all_to_all x1, blocking collectives, summed_on_arrival(): lax.all_to_all(parts, axis, split_axis=0, concat_axis=0, tiled=True)  32.5 us
    ppermute x4, starting transfers between devices, passed_along(): lax.ppermute(value, axis, [(source, source + steps) for source in range(f...  12.5 us
  transfers between devices with their start and end apart: 4, of which 3 were waited for; matrix products, arithmetic and copies ran while one was open for 0% of the time, Pallas kernels for 0%

profile of v1, /device:TPU:96, one launch (start us, length us, event | category | flops | bytes accessed | tf_op | source)
XLA Modules:
  0.0 237.0 jit_solution(8332783350758990716)
XLA Ops:
  0.0 0.0 copy-start
  0.0 2.3 pad_maximum_fusion
  2.3 42.5 %all_to_all.10 = f32[2,1,448,896]{3,2,1,0:T(8,128)S(1)} all-to-all(f32[2,1,448,896]{3,2,1,0:T(8,128)S(1)} %pad_maximum_fusion), channel_id=1, replica_groups=mesh['energy'=128,'mode'=2] {'mode'}, dimensions={0} | all-to-all | bytes 6422528 | tf_op jit(solution)/shard_map/all_to_all | solution.py:49
  44.8 5.0 %collective-permute-start = (f32[1,896,896]{2,1,0:T(8,128)S(1)}, f32[1,896,896]{2,1,0:T(8,128)S(1)}, u32[]{:S(2)}, u32[]{:S(2)}) collective-permute-start(f32[1,896,896]{2,1,0:T(8,128)S(1)} %bitcast.30), channel_id=1, source_target_pairs={{0,4},{2,6},{4,8},{6,10},{8,12},{10,14},{12,16},{14,18},{16,20},{1... | collective-permute-start | bytes 9633800 | tf_op jit(solution)/shard_map/ppermute | solution.py:12
  49.8 1.9 collective-permute-start.1
  51.8 3.6 %collective-permute-start.2 = (f32[1,896,896]{2,1,0:T(8,128)S(1)}, f32[1,896,896]{2,1,0:T(8,128)S(1)}, u32[]{:S(2)}, u32[]{:S(2)}) collective-permute-start(f32[1,896,896]{2,1,0:T(8,128)S(1)} %bitcast.32), channel_id=1, source_target_pairs={{2,0},{4,2},{6,4},{8,6},{10,8},{12,10},{14,12},{16,14},{18,16},{20... | collective-permute-start | bytes 9633800 | tf_op jit(solution)/shard_map/ppermute | solution.py:12
  55.4 1.9 collective-permute-start.3
  58.6 61.1 %collective-permute-done = f32[1,896,896]{2,1,0:T(8,128)S(1)} collective-permute-done((f32[1,896,896]{2,1,0:T(8,128)S(1)}, f32[1,896,896]{2,1,0:T(8,128)S(1)}, u32[]{:S(2)}, u32[]{:S(2)}) %collective-permute-start) | collective-permute-done | bytes 3211296 | tf_op jit(solution)/shard_map/ppermute | solution.py:12
  119.8 0.2 constant_dynamic-update-slice_fusion.4
  120.0 31.2 %collective-permute-done.1 = f32[1,896,896]{2,1,0:T(8,128)S(1)} collective-permute-done((f32[1,896,896]{2,1,0:T(8,128)S(1)}, f32[1,896,896]{2,1,0:T(8,128)S(1)}, u32[]{:S(2)}, u32[]{:S(2)}) %collective-permute-start.1) | collective-permute-done | bytes 3211296 | tf_op jit(solution)/shard_map/ppermute | solution.py:12
  151.1 0.2 constant_dynamic-update-slice_fusion.3
  151.4 0.2 constant_dynamic-update-slice_fusion.2
  151.6 0.0 collective-permute-done.2
  151.6 0.2 constant_dynamic-update-slice_fusion.1
  151.8 10.6 %collective-permute-done.3 = f32[1,896,896]{2,1,0:T(8,128)S(1)} collective-permute-done((f32[1,896,896]{2,1,0:T(8,128)S(1)}, f32[1,896,896]{2,1,0:T(8,128)S(1)}, u32[]{:S(2)}, u32[]{:S(2)}) %collective-permute-start.3) | collective-permute-done | bytes 3211296 | tf_op jit(solution)/shard_map/ppermute | solution.py:12
  162.4 0.2 constant_dynamic-update-slice_fusion
  162.6 34.3 %fusion = bf16[1,896,896]{2,0,1:T(2,128)(2,1)S(1)} fusion(f32[5,896,896]{2,1,0:T(8,128)S(1)} %constant_dynamic-update-slice_fusion, f32[]{:T(128)} %bitcast.3, s32[]{:T(128)} %bitcast.2, f32[]{:T(128)} %bitcast.1, s32[]{:T(128)} %bitcast), kind=kOutput, calls=%fused_computation | convolution fusion | flops 48168984 | bytes 17661968 | tf_op jit(solution)/shard_map/mew,wij->meij/dot_general | solution.py:61
  196.9 0.0 copy-done
  196.9 2.0 convolution_convert_fusion
  198.9 2.0 convolution_bitcast_fusion
  200.9 32.5 %all_to_all.11 = f32[2,1,448,896]{3,2,1,0:T(8,128)} all-to-all(f32[2,1,448,896]{3,2,1,0:T(8,128)S(1)} %convolution_bitcast_fusion), channel_id=1, replica_groups=mesh['energy'=128,'mode'=2] {'mode'}, dimensions={0} | all-to-all | bytes 6422528 | tf_op jit(solution)/shard_map/all_to_all | solution.py:23
  233.5 2.3 reduce_sum.9
  235.7 1.3 multiply_bitcast_fusion
Async XLA Ops:
  0.0 196.9 %copy-start = (bf16[1,896,896]{2,1,0:T(8,128)(2,1)S(1)}, bf16[1,896,896]{2,1,0:T(8,128)(2,1)}, u32[]{:S(2)}) copy-start(bf16[1,896,896]{2,1,0:T(8,128)(2,1)} %param.5) | copy-start | bytes 4816900
  44.8 75.0 %collective-permute-start = (f32[1,896,896]{2,1,0:T(8,128)S(1)}, f32[1,896,896]{2,1,0:T(8,128)S(1)}, u32[]{:S(2)}, u32[]{:S(2)}) collective-permute-start(f32[1,896,896]{2,1,0:T(8,128)S(1)} %bitcast.30), channel_id=1, source_target_pairs={{0,4},{2,6},{4,8},{6,10},{8,12},{10,14},{12,16},{14,18},{16,20},{1... | collective-permute-start | bytes 9633800 | tf_op jit(solution)/shard_map/ppermute | solution.py:12
  49.8 101.3 %collective-permute-start.1 = (f32[1,896,896]{2,1,0:T(8,128)S(1)}, f32[1,896,896]{2,1,0:T(8,128)S(1)}, u32[]{:S(2)}, u32[]{:S(2)}) collective-permute-start(f32[1,896,896]{2,1,0:T(8,128)S(1)} %bitcast.31), channel_id=1, source_target_pairs={{0,2},{2,4},{4,6},{6,8},{8,10},{10,12},{12,14},{14,16},{16,18},{18... | collective-permute-start | bytes 9633800 | tf_op jit(solution)/shard_map/ppermute | solution.py:12
  51.8 99.8 %collective-permute-start.2 = (f32[1,896,896]{2,1,0:T(8,128)S(1)}, f32[1,896,896]{2,1,0:T(8,128)S(1)}, u32[]{:S(2)}, u32[]{:S(2)}) collective-permute-start(f32[1,896,896]{2,1,0:T(8,128)S(1)} %bitcast.32), channel_id=1, source_target_pairs={{2,0},{4,2},{6,4},{8,6},{10,8},{12,10},{14,12},{16,14},{18,16},{20... | collective-permute-start | bytes 9633800 | tf_op jit(solution)/shard_map/ppermute | solution.py:12
  55.4 107.0 %collective-permute-start.3 = (f32[1,896,896]{2,1,0:T(8,128)S(1)}, f32[1,896,896]{2,1,0:T(8,128)S(1)}, u32[]{:S(2)}, u32[]{:S(2)}) collective-permute-start(f32[1,896,896]{2,1,0:T(8,128)S(1)} %bitcast.33), channel_id=1, source_target_pairs={{4,0},{6,2},{8,4},{10,6},{12,8},{14,10},{16,12},{18,14},{20,16},{2... | collective-permute-start | bytes 9633800 | tf_op jit(solution)/shard_map/ppermute | solution.py:12
